TPU v7x, 32 devices: a whole 2x2x4 slice. The times are simulated.
32 devices in a mesh: tensor: 4 (over z), dp: 4 (over y, x), replica: 2 (over core).
Axes of the slice: x: 2, y: 2, z: 4, core: 2. Of those that a mesh axis runs over, the one named last changes fastest.
Arguments:
- states: bfloat16 [8, 256, 4096], P(('dp', 'replica')), may hold values from -6 to 6
- norm_gain: float32 [4096], replicated, may hold values from 0.26 to 4.4
- gate_up: bfloat16 [4096, 2, 14336], P('replica', None, 'tensor'), may hold values from -0.09375 to 0.09375
- cotangent: bfloat16 [8, 256, 14336], P(('dp', 'replica'), None, 'tensor'), may hold values from -120 to 120
- prompt: bfloat16 [32, 4096], replicated, may hold values from -6 to 6
- step_sizes: float32 [3], replicated, may hold values from 0.3 to 1
- insert_at: int32 [8], P(('dp', 'replica')), may hold values from 0 to 224, as said below
- lengths: int32 [8], P(('dp', 'replica')), may hold values from 128 to 256, as said below
Outputs:
- prompt_final: float32 [32, 4096], P(None, 'tensor')
- weight_step: bfloat16 [4096, 2, 14336], P(('dp', 'replica'), None, 'tensor')
Inputs may be any that keep to these rules, and one draw needn't show every extreme that they name: Each prompt lies inside its sequence: insert_at[b] + 32 <= lengths[b]; in every draw some prompt begins at row 0 and some prompt ends at the last row 255. `lengths`: in every draw some sequence has all 256 rows live and some has 128.
All inputs are finite; a program needn't handle non-finite values.
Results may differ from a plain program's by a relative error of at most 0.012.
Values may be sent and summed in bfloat16 or wider, within the bound.
A program may use at most 320 MiB of HBM per device.

v0:
```python
import jax
import jax.numpy as jnp
from jax import lax
from jax.sharding import PartitionSpec as P

D = 4096
FF = 14336


def row_scale(feature_rows):
    return lax.rsqrt(jnp.mean(feature_rows * feature_rows, axis=-1, keepdims=True) + 1e-05)


def silu_parts(gate_values):
    sigmoid_value = jax.nn.sigmoid(gate_values)
    return (
        gate_values * sigmoid_value,
        sigmoid_value * (1.0 + gate_values * (1.0 - sigmoid_value)),
    )


def hidden_grads(normalized, weight_pair, cotan_rows):
    unit_count = weight_pair.shape[1] // 2
    projected = jnp.dot(normalized, weight_pair, preferred_element_type=jnp.float32)
    activated, derivative = silu_parts(projected[:, :unit_count])
    up_part = projected[:, unit_count:]
    return jnp.concatenate(
        [cotan_rows * up_part * derivative, cotan_rows * activated], axis=1
    ).astype(jnp.bfloat16)


def norm_back(shifted, inverse_rms, norm_gain, feature_grad):
    feature_mean = jnp.mean(shifted * norm_gain * feature_grad, axis=-1, keepdims=True)
    return (
        inverse_rms * norm_gain * feature_grad
        - shifted * (inverse_rms * inverse_rms * inverse_rms) * feature_mean
    )


def per_device(states, norm_gain, gate_up, cotangent, prompt, step_sizes, insert_at, lengths):
    gathered = lax.all_gather(gate_up, "replica", axis=0, tiled=True)
    feature_count = gathered.shape[0]
    unit_count = gathered.shape[2]
    weight_pair = gathered.reshape(feature_count, 2 * unit_count)
    seq_states = states[0]
    seq_cotan = cotangent[0].astype(jnp.float32)
    prompt_start = insert_at[0]
    seq_length = lengths[0]
    prompt_count = prompt.shape[0]
    prompt_base = lax.dynamic_slice_in_dim(seq_states, prompt_start, prompt_count, 0).astype(
        jnp.float32
    )
    prompt_cotan = lax.dynamic_slice_in_dim(seq_cotan, prompt_start, prompt_count, 0)
    adversary = prompt.astype(jnp.float32)
    for attack_step in range(step_sizes.shape[0]):
        shifted = prompt_base + adversary
        inverse_rms = row_scale(shifted)
        normalized = (shifted * inverse_rms * norm_gain).astype(jnp.bfloat16)
        unit_grads = hidden_grads(normalized, weight_pair, prompt_cotan)
        feature_grad = lax.dot_general(
            unit_grads, weight_pair, (((1,), (1,)), ((), ())), preferred_element_type=jnp.float32
        )
        feature_grad = lax.psum(feature_grad, "tensor")
        summed_grad = lax.psum(
            norm_back(shifted, inverse_rms, norm_gain, feature_grad), ("dp", "replica")
        )
        adversary = adversary + step_sizes[attack_step] * summed_grad * lax.rsqrt(
            jnp.mean(summed_grad * summed_grad, axis=-1, keepdims=True) + 1e-06
        )
    full_rows = lax.dynamic_update_slice_in_dim(
        seq_states.astype(jnp.float32), prompt_base + adversary, prompt_start, 0
    )
    full_normed = (full_rows * row_scale(full_rows) * norm_gain).astype(jnp.bfloat16)
    positions = lax.broadcasted_iota(jnp.int32, (full_rows.shape[0], 1), 0)
    live_cotan = jnp.where(positions < seq_length, seq_cotan, 0.0)
    token_grads = hidden_grads(full_normed, weight_pair, live_cotan)
    received = lax.all_to_all(
        full_normed, ("dp", "replica"), split_axis=1, concat_axis=0, tiled=True
    )
    weight_grad = lax.dot_general(
        received,
        lax.all_gather(token_grads, ("dp", "replica"), axis=0, tiled=True),
        (((0,), (0,)), ((), ())),
        preferred_element_type=jnp.float32,
    )
    squares = lax.psum(jnp.sum(weight_grad * weight_grad), ("tensor", "dp", "replica"))
    weight_step = (weight_grad * lax.rsqrt(squares / (2 * D * FF) + 1e-06)).astype(jnp.bfloat16)
    weight_step = weight_step.reshape(weight_grad.shape[0], 2, unit_count)
    column_count = adversary.shape[1] // lax.axis_size("tensor")
    prompt_final = lax.dynamic_slice_in_dim(
        adversary, lax.axis_index("tensor") * column_count, column_count, 1
    )
    return (prompt_final, weight_step)


def solution(mesh):
    return jax.shard_map(
        per_device,
        mesh=mesh,
        in_specs=(
            P(("dp", "replica"), None, None),
            P(),
            P("replica", None, "tensor"),
            P(("dp", "replica"), None, "tensor"),
            P(),
            P(),
            P(("dp", "replica")),
            P(("dp", "replica")),
        ),
        out_specs=(P(None, "tensor"), P(("dp", "replica"), None, "tensor")),
        check_vma=False,
    )
```

profile of v0, /device:TPU:0, one launch (start us, length us, event | category | flops | bytes accessed | tf_op | source)
XLA Modules:
  0.0 889.3 jit_solution(5123396470353676943)
XLA Ops:
  8.8 3.8 convert_element_type.43
  12.8 83.6 %all-gather.3.cloned.1.call-done = bf16[4096,2,3584]{2,1,0:T(2,128)(2,1)} async-done(((bf16[2048,2,3584]{2,1,0:T(2,128)(2,1)}), bf16[4096,2,3584]{2,1,0:T(2,128)(2,1)}) %all-gather.3.cloned.1.call-update) | async-done | bytes 58720272 | tf_op jit(solution)/shard_map/all_gather | solution.py:41
  96.4 39.3 %copy.16 = bf16[512,8,2,3584]{3,1,2,0:T(8,128)(2,1)} copy(bf16[512,8,2,3584]{3,2,1,0:T(2,128)(2,1)} %bitcast.75) | data formatting | bytes 117440512
  135.7 21.5 %fusion.23 = f32[32,7168]{1,0:T(8,128)S(1)} fusion(bf16[4096,7168]{1,0:T(8,128)(2,1)} %bitcast.68, bf16[32,4096]{1,0:T(8,128)(2,1)S(1)} %copy-done.2, f32[4096]{0:T(1024)S(1)} %copy-done.5, f32[32]{0:T(128)S(1)} %get-tuple-element.24, bf16[1,256,4096]{2,1,0:T(8,128)(2,1)S(1)} %copy-done.1, s32[]{:T(128)S(6)} %select_n.12), kind=kOutput, calls=%fused_computation.64 | convolution fusion | flops 1879834624 | bytes 60178948 | tf_op jit(solution)/shard_map/dot_general | solution.py:24
  158.5 24.7 %fusion.8 = f32[32,4096]{1,0:T(8,128)} fusion(bf16[4096,7168]{1,0:T(8,128)(2,1)} %bitcast.69, bf16[32,3584]{1,0:T(8,128)(2,1)S(1)} %get-tuple-element.15, bf16[32,3584]{1,0:T(8,128)(2,1)S(1)} %get-tuple-element.14), kind=kOutput, calls=%fused_computation.43 | convolution fusion | flops 1879965696 | bytes 59703296 | tf_op jit(solution)/shard_map/dot_general | solution.py:60
  183.3 39.6 %all-reduce.7.cloned.1.call-done = f32[32,4096]{1,0:T(8,128)} async-done(((f32[32,4096]{1,0:T(8,128)}), f32[32,4096]{1,0:T(8,128)}) %all-reduce.7.cloned.1.call-update) | async-done | bytes 524304 | tf_op jit(solution)/shard_map/psum | solution.py:63
  226.9 54.0 %all-reduce.9.cloned.1.call-done = f32[32,4096]{1,0:T(8,128)} async-done(((f32[32,4096]{1,0:T(8,128)}), f32[32,4096]{1,0:T(8,128)}) %all-reduce.9.cloned.1.call-update) | async-done | bytes 524304 | tf_op jit(solution)/shard_map/psum | solution.py:64
  284.0 21.5 %fusion.24 = f32[32,7168]{1,0:T(8,128)S(1)} fusion(bf16[4096,7168]{1,0:T(8,128)(2,1)} %bitcast.70, f32[32,4096]{1,0:T(8,128)S(1)} %get-tuple-element.7, f32[32]{0:T(128)S(1)} %get-tuple-element.22, f32[4096]{0:T(1024)S(1)} %copy-done.5), kind=kOutput, calls=%fused_computation.65 | convolution fusion | flops 1879441408 | bytes 60178560 | tf_op jit(solution)/shard_map/dot_general | solution.py:24
  306.9 24.7 %fusion.12 = f32[32,4096]{1,0:T(8,128)} fusion(bf16[4096,7168]{1,0:T(8,128)(2,1)} %bitcast.71, bf16[32,3584]{1,0:T(8,128)(2,1)S(1)} %get-tuple-element.13, bf16[32,3584]{1,0:T(8,128)(2,1)S(1)} %get-tuple-element.12), kind=kOutput, calls=%fused_computation.47 | convolution fusion | flops 1879965696 | bytes 59703296 | tf_op jit(solution)/shard_map/dot_general | solution.py:60
  331.6 37.7 %all-reduce.11.cloned.1.call-done = f32[32,4096]{1,0:T(8,128)} async-done(((f32[32,4096]{1,0:T(8,128)}), f32[32,4096]{1,0:T(8,128)}) %all-reduce.11.cloned.1.call-update) | async-done | bytes 524304 | tf_op jit(solution)/shard_map/psum | solution.py:63
  372.9 54.4 %all-reduce.13.cloned.1.call-done = f32[32,4096]{1,0:T(8,128)} async-done(((f32[32,4096]{1,0:T(8,128)}), f32[32,4096]{1,0:T(8,128)}) %all-reduce.13.cloned.1.call-update) | async-done | bytes 524304 | tf_op jit(solution)/shard_map/psum | solution.py:64
  428.5 2.6 multiply_reduce_fusion.4
  431.1 21.4 %fusion.25 = f32[32,7168]{1,0:T(8,128)S(1)} fusion(bf16[4096,7168]{1,0:T(8,128)(2,1)} %bitcast.72, f32[32]{0:T(128)S(1)} %get-tuple-element.20, f32[4096]{0:T(1024)S(1)} %copy-done.5, f32[32,4096]{1,0:T(8,128)S(1)} %get-tuple-element.5, bf16[1,256,4096]{2,1,0:T(8,128)(2,1)S(1)} %copy-done.1, s32[]{:T(128)S(6)} %select_n.12), kind=kOutput, calls=%fused_computation.66 | convolution fusion | flops 1879703552 | bytes 60441092 | tf_op jit(solution)/shard_map/dot_general | solution.py:24
  453.8 24.7 %fusion.16 = f32[32,4096]{1,0:T(8,128)} fusion(bf16[4096,7168]{1,0:T(8,128)(2,1)} %bitcast.73, bf16[32,3584]{1,0:T(8,128)(2,1)S(1)} %get-tuple-element.11, bf16[32,3584]{1,0:T(8,128)(2,1)S(1)} %get-tuple-element.10), kind=kOutput, calls=%fused_computation.51 | convolution fusion | flops 1879965696 | bytes 59703296 | tf_op jit(solution)/shard_map/dot_general | solution.py:60
  478.6 2.5 copy.13
  481.1 35.2 %all-reduce.15.cloned.1.call-done = f32[32,4096]{1,0:T(8,128)} async-done(((f32[32,4096]{1,0:T(8,128)}), f32[32,4096]{1,0:T(8,128)}) %all-reduce.15.cloned.1.call-update) | async-done | bytes 524304 | tf_op jit(solution)/shard_map/psum | solution.py:63
  520.2 3.9 bitcast_convert_fusion
  524.8 49.5 %all-reduce.17.cloned.1.call-done = f32[32,4096]{1,0:T(8,128)} async-done(((f32[32,4096]{1,0:T(8,128)}), f32[32,4096]{1,0:T(8,128)}) %all-reduce.17.cloned.1.call-update) | async-done | bytes 524304 | tf_op jit(solution)/shard_map/psum | solution.py:64
  575.5 2.7 convert_add_fusion
  578.8 11.9 %dynamic_update_slice.3 = f32[256,4096]{0,1:T(8,128)} dynamic-update-slice(f32[256,4096]{0,1:T(8,128)} %bitcast_convert_fusion, f32[32,4096]{0,1:T(8,128)S(1)} %copy.14, s32[]{:T(128)S(6)} %select_n.12, s32[]{:T(128)} %constant.15.clone.1) | dynamic-update-slice | bytes 1048580 | tf_op jit(solution)/shard_map/dynamic_update_slice | solution.py:70
  590.7 2.9 multiply_reduce_fusion.1
  595.9 28.3 %fusion.39 = f32[256,7168]{1,0:T(8,128)} fusion(bf16[256,4096]{0,1:T(8,128)(2,1)} %multiply_convert_fusion.1, bf16[4096,7168]{1,0:T(8,128)(2,1)} %bitcast.74), kind=kOutput, calls=%fused_computation.95 | convolution fusion | flops 15032385536 | bytes 68157440 | tf_op jit(solution)/shard_map/dot_general | solution.py:24
  624.2 4.1 fusion.1
  628.3 2.3 pad_maximum_fusion
  630.6 3.8 all-to-all-start
  636.0 41.6 %all-to-all-done = bf16[256,8,512]{0,2,1:T(8,128)(2,1)S(1)} async-done(((bf16[256,8,512]{0,2,1:T(8,128)(2,1)}), bf16[256,8,512]{0,2,1:T(8,128)(2,1)S(1)}, u32[]{:S(2)}, u32[]{:S(2)}) %all-to-all-start) | async-done | bytes 2097184 | tf_op jit(solution)/shard_map/all_to_all | solution.py:77
  677.6 2.4 copy.15
  680.0 109.1 %all-gather.5.cloned.1.call-done = bf16[2048,7168]{1,0:T(8,128)(2,1)} async-done(((bf16[256,7168]{1,0:T(8,128)(2,1)}), bf16[2048,7168]{1,0:T(8,128)(2,1)}) %all-gather.5.cloned.1.call-update) | async-done | bytes 29360144 | tf_op jit(solution)/shard_map/all_gather | solution.py:82
  789.1 26.1 %multiply_reduce_fusion = (f32[]{:T(128)}, f32[512,7168]{1,0:T(8,128)}) fusion(bf16[2048,512]{1,0:T(8,128)(2,1)} %bitcast.77, bf16[2048,7168]{1,0:T(8,128)(2,1)} %all-gather.5.cloned.1.call-done), kind=kOutput, calls=%fused_computation.1 | convolution fusion | flops 15039725568 | bytes 46137348 | tf_op jit(solution)/shard_map/dot_general | solution.py:80
  815.2 39.7 %psum.55 = f32[]{:T(128)} all-reduce(f32[]{:T(128)} %get-tuple-element.25), channel_id=1, replica_groups=mesh['tensor'=4,'dp'=4,'replica'=2] {'tensor','dp','replica'}, use_global_device_ids=true, to_apply=%region_17.18 | all-reduce | flops 1 | bytes 8 | tf_op jit(solution)/shard_map/psum | solution.py:86
  855.6 9.8 %multiply_convert_fusion = bf16[512,7168]{1,0:T(8,128)(2,1)} fusion(f32[512,7168]{1,0:T(8,128)} %get-tuple-element.26, f32[]{:T(128)S(6)} %rsqrt.75), kind=kLoop, calls=%fused_computation | loop fusion | flops 7340032 | bytes 22020100 | tf_op jit(solution)/shard_map/convert_element_type | solution.py:87
  865.4 16.9 %reshape.113 = bf16[512,2,3584]{2,1,0:T(2,128)(2,1)} reshape(bf16[512,7168]{1,0:T(8,128)(2,1)} %multiply_convert_fusion) | data formatting | bytes 14680064 | tf_op jit(solution)/shard_map/reshape | solution.py:88
  (59 shorter events, 26.6 us)
Async XLA Ops:
  7.2 89.3 %all-gather.3.cloned.1.call-start = ((), (), s32[]{:S(2)}) async-start(), calls=%async_computation.1 | async-start | bytes 88080384 | tf_op jit(solution)/shard_map/all_gather | solution.py:41
  7.9 4.6 copy-start.1
  7.9 4.6 copy-start.2
  7.9 214.9 %all-reduce.7.cloned.1.call-start = ((), (), s32[]{:S(2)}) async-start(), calls=%async_computation.2 | async-start | bytes 1048576 | tf_op jit(solution)/shard_map/psum | solution.py:63
  96.4 39.3 %copy-start.5 = (f32[4096]{0:T(1024)S(1)}, f32[4096]{0:T(1024)}, u32[]{:S(2)}) copy-start(f32[4096]{0:T(1024)} %param.9) | copy-start | bytes 49156
  183.2 43.0 %copy-start.6 = (f32[3]{0:T(128)S(1)}, f32[3]{0:T(128)}, u32[]{:S(2)}) copy-start(f32[3]{0:T(128)} %param.13) | copy-start | bytes 40
  183.3 97.6 %all-reduce.9.cloned.1.call-start = ((), (), s32[]{:S(2)}) async-start(), calls=%async_computation.3 | async-start | bytes 1048576 | tf_op jit(solution)/shard_map/psum | solution.py:64
  226.2 143.1 %all-reduce.11.cloned.1.call-start = ((), (), s32[]{:S(2)}) async-start(), calls=%async_computation.4 | async-start | bytes 1048576 | tf_op jit(solution)/shard_map/psum | solution.py:63
  331.5 96.9 %copy-start.4 = (f32[32,4096]{1,0:T(8,128)S(1)}, f32[32,4096]{1,0:T(8,128)}, u32[]{:S(2)}) copy-start(f32[32,4096]{1,0:T(8,128)} %all-reduce.9.cloned.1.call-done) | copy-start | bytes 1572868
  331.6 95.7 %all-reduce.13.cloned.1.call-start = ((), (), s32[]{:S(2)}) async-start(), calls=%async_computation.5 | async-start | bytes 1048576 | tf_op jit(solution)/shard_map/psum | solution.py:64
  372.6 143.8 %all-reduce.15.cloned.1.call-start = ((), (), s32[]{:S(2)}) async-start(), calls=%async_computation.6 | async-start | bytes 1048576 | tf_op jit(solution)/shard_map/psum | solution.py:63
  478.6 95.8 %all-reduce.17.cloned.1.call-start = ((), (), s32[]{:S(2)}) async-start(), calls=%async_computation.7 | async-start | bytes 1048576 | tf_op jit(solution)/shard_map/psum | solution.py:64
  519.6 269.4 %all-gather.5.cloned.1.call-start = ((), (), s32[]{:S(2)}) async-start(), calls=%async_computation.8 | async-start | bytes 33030144 | tf_op jit(solution)/shard_map/all_gather | solution.py:82
  590.7 3.4 copy-start
  595.9 28.3 %copy-start.3 = (bf16[1,256,3584]{2,1,0:T(8,128)(2,1)S(1)}, bf16[1,256,3584]{2,1,0:T(8,128)(2,1)}, u32[]{:S(2)}) copy-start(bf16[1,256,3584]{2,1,0:T(8,128)(2,1)} %param.11) | copy-start | bytes 5505028
  630.6 47.0 %all-to-all-start = ((bf16[256,8,512]{0,2,1:T(8,128)(2,1)}), bf16[256,8,512]{0,2,1:T(8,128)(2,1)S(1)}, u32[]{:S(2)}, u32[]{:S(2)}) async-start(bf16[256,8,512]{0,2,1:T(8,128)(2,1)} %bitcast.8), calls=%async_computation | async-start | bytes 4194304 | tf_op jit(solution)/shard_map/all_to_all | solution.py:77
Sparse Core Ops, SparseCore 0:
  9.5 86.8 all-gather.2
  183.4 39.4 all-reduce.6
  226.3 54.5 all-reduce.8
  331.7 37.5 all-reduce.10
  372.7 54.5 all-reduce.12
  478.7 37.5 all-reduce.14
  519.8 54.5 all-reduce.16
  630.7 158.2 all-gather.4
where the time goes:
time: 900 us; the launch traced here: 889 us
  waiting for transfers between devices  505 us (56%)
  matrix products  193 us (21%)
  local copies, waits for them, and re-layouts  76.3 us (8%)
  other arithmetic  53.3 us (6%)
  blocking collectives  39.7 us (4%)
  between operations  16.6 us (2%)
    psum x3, waiting for transfers between devices, per_device(): lax.psum(norm_back(shifted, inverse_rms, norm_gain, feature_grad), ('dp',...  158 us
    psum x3, waiting for transfers between devices, per_device(): feature_grad = lax.psum(feature_grad, 'tensor')  112 us
    all_gather x1, waiting for transfers between devices, per_device(): lax.all_gather(token_grads, ('dp', 'replica'), axis=0, tiled=True)  109 us
    dot_general x4, matrix products, hidden_grads(): jnp.dot(normalized, weight_pair, preferred_element_type=jnp.float32)  92.8 us
    all_gather x1, waiting for transfers between devices, per_device(): gathered = lax.all_gather(gate_up, 'replica', axis=0, tiled=True)  83.6 us
    dot_general x3, matrix products, per_device(): lax.dot_general(unit_grads, weight_pair, (((1,), (1,)), ((), ())), prefer...  74.1 us
    unnamed x16, local copies, waits for them, and re-layouts  42.3 us
    all_to_all x1, waiting for transfers between devices, per_device(): lax.all_to_all(full_normed, ('dp', 'replica'), split_axis=1, concat_axis=...  41.6 us
  transfers between devices with their start and end apart: 9, of which 9 were waited for; matrix products, arithmetic and copies ran while one was open for 2% of the time, Pallas kernels for 0%

commit v1 on v0

--- a/solution.py
+++ b/solution.py
@@ -62,7 +62,7 @@
         )
         feature_grad = lax.psum(feature_grad, "tensor")
         summed_grad = lax.psum(
-            norm_back(shifted, inverse_rms, norm_gain, feature_grad), ("dp", "replica")
+            lax.psum(norm_back(shifted, inverse_rms, norm_gain, feature_grad), "replica"), "dp"
         )
         adversary = adversary + step_sizes[attack_step] * summed_grad * lax.rsqrt(
             jnp.mean(summed_grad * summed_grad, axis=-1, keepdims=True) + 1e-06

time: 900 us -> 942 us (1.047)
  waiting for transfers between devices: 505 us -> 548 us
    psum x3 -> x6, waiting for transfers between devices: 158 us -> 197 us  [the longest x3 143 us: per_device(): lax.psum(lax.psum(norm_back(shifted, inverse_rms, norm_gain, feature_grad...]
  transfers between devices with their start and end apart: 9 -> 12, of which waited for: 9 -> 12; matrix products, arithmetic and copies ran while one was open for 2% -> 2% of each run, Pallas kernels for 0% -> 0%
where the time goes in v1:
time: 942 us; the launch traced here: 932 us
  waiting for transfers between devices  548 us (58%)
  matrix products  193 us (20%)
  local copies, waits for them, and re-layouts  76.3 us (8%)
  other arithmetic  53.4 us (6%)
  blocking collectives  39.7 us (4%)
  between operations  16.4 us (2%)
    psum x3, waiting for transfers between devices, per_device(): lax.psum(lax.psum(norm_back(shifted, inverse_rms, norm_gain, feature_grad...  143 us
    psum x3, waiting for transfers between devices, per_device(): feature_grad = lax.psum(feature_grad, 'tensor')  116 us
    all_gather x1, waiting for transfers between devices, per_device(): lax.all_gather(token_grads, ('dp', 'replica'), axis=0, tiled=True)  110 us
    dot_general x4, matrix products, hidden_grads(): jnp.dot(normalized, weight_pair, preferred_element_type=jnp.float32)  92.8 us
    all_gather x1, waiting for transfers between devices, per_device(): gathered = lax.all_gather(gate_up, 'replica', axis=0, tiled=True)  83.6 us
    dot_general x3, matrix products, per_device(): lax.dot_general(unit_grads, weight_pair, (((1,), (1,)), ((), ())), prefer...  74.1 us
    psum x3, waiting for transfers between devices, per_device(): lax.psum(norm_back(shifted, inverse_rms, norm_gain, feature_grad), 'repli...  53.9 us
    unnamed x16, local copies, waits for them, and re-layouts  42.3 us
  transfers between devices with their start and end apart: 12, of which 12 were waited for; matrix products, arithmetic and copies ran while one was open for 2% of the time, Pallas kernels for 0%

profile of v1, /device:TPU:0, one launch (start us, length us, event | category | flops | bytes accessed | tf_op | source)
XLA Modules:
  0.0 932.1 jit_solution(11572833854644070070)
XLA Ops:
  8.8 3.8 convert_element_type.43
  12.8 83.6 %all-gather.3.cloned.1.call-done = bf16[4096,2,3584]{2,1,0:T(2,128)(2,1)} async-done(((bf16[2048,2,3584]{2,1,0:T(2,128)(2,1)}), bf16[4096,2,3584]{2,1,0:T(2,128)(2,1)}) %all-gather.3.cloned.1.call-update) | async-done | bytes 58720272 | tf_op jit(solution)/shard_map/all_gather | solution.py:41
  96.4 39.3 %copy.16 = bf16[512,8,2,3584]{3,1,2,0:T(8,128)(2,1)} copy(bf16[512,8,2,3584]{3,2,1,0:T(2,128)(2,1)} %bitcast.75) | data formatting | bytes 117440512
  135.7 21.5 %fusion.23 = f32[32,7168]{1,0:T(8,128)S(1)} fusion(bf16[4096,7168]{1,0:T(8,128)(2,1)} %bitcast.68, bf16[32,4096]{1,0:T(8,128)(2,1)S(1)} %copy-done.2, f32[4096]{0:T(1024)S(1)} %copy-done.5, f32[32]{0:T(128)S(1)} %get-tuple-element.24, bf16[1,256,4096]{2,1,0:T(8,128)(2,1)S(1)} %copy-done.1, s32[]{:T(128)S(6)} %select_n.12), kind=kOutput, calls=%fused_computation.64 | convolution fusion | flops 1879834624 | bytes 60178948 | tf_op jit(solution)/shard_map/dot_general | solution.py:24
  158.5 24.7 %fusion.8 = f32[32,4096]{1,0:T(8,128)} fusion(bf16[4096,7168]{1,0:T(8,128)(2,1)} %bitcast.69, bf16[32,3584]{1,0:T(8,128)(2,1)S(1)} %get-tuple-element.15, bf16[32,3584]{1,0:T(8,128)(2,1)S(1)} %get-tuple-element.14), kind=kOutput, calls=%fused_computation.43 | convolution fusion | flops 1879965696 | bytes 59703296 | tf_op jit(solution)/shard_map/dot_general | solution.py:60
  183.3 39.6 %all-reduce.10.cloned.1.call-done = f32[32,4096]{1,0:T(8,128)} async-done(((f32[32,4096]{1,0:T(8,128)}), f32[32,4096]{1,0:T(8,128)}) %all-reduce.10.cloned.1.call-update) | async-done | bytes 524304 | tf_op jit(solution)/shard_map/psum | solution.py:63
  226.3 18.8 %all-reduce.12.cloned.1.call-done = f32[32,4096]{1,0:T(8,128)} async-done(((f32[32,4096]{1,0:T(8,128)}), f32[32,4096]{1,0:T(8,128)}) %all-reduce.12.cloned.1.call-update) | async-done | bytes 524304 | tf_op jit(solution)/shard_map/psum | solution.py:65
  245.8 49.0 %all-reduce.14.cloned.1.call-done = f32[32,4096]{1,0:T(8,128)} async-done(((f32[32,4096]{1,0:T(8,128)}), f32[32,4096]{1,0:T(8,128)}) %all-reduce.14.cloned.1.call-update) | async-done | bytes 524304 | tf_op jit(solution)/shard_map/psum | solution.py:64
  298.0 21.5 %fusion.24 = f32[32,7168]{1,0:T(8,128)S(1)} fusion(bf16[4096,7168]{1,0:T(8,128)(2,1)} %bitcast.70, f32[32,4096]{1,0:T(8,128)S(1)} %get-tuple-element.7, f32[32]{0:T(128)S(1)} %get-tuple-element.22, f32[4096]{0:T(1024)S(1)} %copy-done.5), kind=kOutput, calls=%fused_computation.65 | convolution fusion | flops 1879441408 | bytes 60178560 | tf_op jit(solution)/shard_map/dot_general | solution.py:24
  320.8 24.7 %fusion.12 = f32[32,4096]{1,0:T(8,128)} fusion(bf16[4096,7168]{1,0:T(8,128)(2,1)} %bitcast.71, bf16[32,3584]{1,0:T(8,128)(2,1)S(1)} %get-tuple-element.13, bf16[32,3584]{1,0:T(8,128)(2,1)S(1)} %get-tuple-element.12), kind=kOutput, calls=%fused_computation.47 | convolution fusion | flops 1879965696 | bytes 59703296 | tf_op jit(solution)/shard_map/dot_general | solution.py:60
  345.6 38.4 %all-reduce.16.cloned.1.call-done = f32[32,4096]{1,0:T(8,128)} async-done(((f32[32,4096]{1,0:T(8,128)}), f32[32,4096]{1,0:T(8,128)}) %all-reduce.16.cloned.1.call-update) | async-done | bytes 524304 | tf_op jit(solution)/shard_map/psum | solution.py:63
  387.3 18.8 %all-reduce.18.cloned.1.call-done = f32[32,4096]{1,0:T(8,128)} async-done(((f32[32,4096]{1,0:T(8,128)}), f32[32,4096]{1,0:T(8,128)}) %all-reduce.18.cloned.1.call-update) | async-done | bytes 524304 | tf_op jit(solution)/shard_map/psum | solution.py:65
  406.5 49.2 %all-reduce.20.cloned.1.call-done = f32[32,4096]{1,0:T(8,128)} async-done(((f32[32,4096]{1,0:T(8,128)}), f32[32,4096]{1,0:T(8,128)}) %all-reduce.20.cloned.1.call-update) | async-done | bytes 524304 | tf_op jit(solution)/shard_map/psum | solution.py:64
  456.8 2.7 multiply_reduce_fusion.4
  459.5 21.4 %fusion.25 = f32[32,7168]{1,0:T(8,128)S(1)} fusion(bf16[4096,7168]{1,0:T(8,128)(2,1)} %bitcast.72, f32[32]{0:T(128)S(1)} %get-tuple-element.20, f32[4096]{0:T(1024)S(1)} %copy-done.5, f32[32,4096]{1,0:T(8,128)S(1)} %get-tuple-element.5, bf16[1,256,4096]{2,1,0:T(8,128)(2,1)S(1)} %copy-done.1, s32[]{:T(128)S(6)} %select_n.12), kind=kOutput, calls=%fused_computation.66 | convolution fusion | flops 1879703552 | bytes 60441092 | tf_op jit(solution)/shard_map/dot_general | solution.py:24
  482.3 24.7 %fusion.16 = f32[32,4096]{1,0:T(8,128)} fusion(bf16[4096,7168]{1,0:T(8,128)(2,1)} %bitcast.73, bf16[32,3584]{1,0:T(8,128)(2,1)S(1)} %get-tuple-element.11, bf16[32,3584]{1,0:T(8,128)(2,1)S(1)} %get-tuple-element.10), kind=kOutput, calls=%fused_computation.51 | convolution fusion | flops 1879965696 | bytes 59703296 | tf_op jit(solution)/shard_map/dot_general | solution.py:60
  507.1 38.4 %all-reduce.22.cloned.1.call-done = f32[32,4096]{1,0:T(8,128)} async-done(((f32[32,4096]{1,0:T(8,128)}), f32[32,4096]{1,0:T(8,128)}) %all-reduce.22.cloned.1.call-update) | async-done | bytes 524304 | tf_op jit(solution)/shard_map/psum | solution.py:63
  551.4 16.3 %all-reduce.24.cloned.1.call-done = f32[32,4096]{1,0:T(8,128)} async-done(((f32[32,4096]{1,0:T(8,128)}), f32[32,4096]{1,0:T(8,128)}) %all-reduce.24.cloned.1.call-update) | async-done | bytes 524304 | tf_op jit(solution)/shard_map/psum | solution.py:65
  568.2 3.9 bitcast_convert_fusion
  572.8 44.5 %all-reduce.26.cloned.1.call-done = f32[32,4096]{1,0:T(8,128)} async-done(((f32[32,4096]{1,0:T(8,128)}), f32[32,4096]{1,0:T(8,128)}) %all-reduce.26.cloned.1.call-update) | async-done | bytes 524304 | tf_op jit(solution)/shard_map/psum | solution.py:64
  618.5 2.7 convert_add_fusion
  621.8 11.9 %dynamic_update_slice.3 = f32[256,4096]{0,1:T(8,128)} dynamic-update-slice(f32[256,4096]{0,1:T(8,128)} %bitcast_convert_fusion, f32[32,4096]{0,1:T(8,128)S(1)} %copy.14, s32[]{:T(128)S(6)} %select_n.12, s32[]{:T(128)} %constant.15.clone.1) | dynamic-update-slice | bytes 1048580 | tf_op jit(solution)/shard_map/dynamic_update_slice | solution.py:70
  633.7 2.9 multiply_reduce_fusion.1
  638.9 28.3 %fusion.39 = f32[256,7168]{1,0:T(8,128)} fusion(bf16[256,4096]{0,1:T(8,128)(2,1)} %multiply_convert_fusion.1, bf16[4096,7168]{1,0:T(8,128)(2,1)} %bitcast.74), kind=kOutput, calls=%fused_computation.95 | convolution fusion | flops 15032385536 | bytes 68157440 | tf_op jit(solution)/shard_map/dot_general | solution.py:24
  667.2 4.1 fusion.1
  673.6 3.8 all-to-all-start
  679.0 41.0 %all-to-all-done = bf16[256,8,512]{0,2,1:T(8,128)(2,1)S(1)} async-done(((bf16[256,8,512]{0,2,1:T(8,128)(2,1)}), bf16[256,8,512]{0,2,1:T(8,128)(2,1)S(1)}, u32[]{:S(2)}, u32[]{:S(2)}) %all-to-all-start) | async-done | bytes 2097184 | tf_op jit(solution)/shard_map/all_to_all | solution.py:77
  722.3 109.8 %all-gather.5.cloned.1.call-done = bf16[2048,7168]{1,0:T(8,128)(2,1)} async-done(((bf16[256,7168]{1,0:T(8,128)(2,1)}), bf16[2048,7168]{1,0:T(8,128)(2,1)}) %all-gather.5.cloned.1.call-update) | async-done | bytes 29360144 | tf_op jit(solution)/shard_map/all_gather | solution.py:82
  832.1 26.1 %multiply_reduce_fusion = (f32[]{:T(128)}, f32[512,7168]{1,0:T(8,128)}) fusion(bf16[2048,512]{1,0:T(8,128)(2,1)} %bitcast.77, bf16[2048,7168]{1,0:T(8,128)(2,1)} %all-gather.5.cloned.1.call-done), kind=kOutput, calls=%fused_computation.1 | convolution fusion | flops 15039725568 | bytes 46137348 | tf_op jit(solution)/shard_map/dot_general | solution.py:80
  858.3 39.7 %psum.79 = f32[]{:T(128)} all-reduce(f32[]{:T(128)} %get-tuple-element.25), channel_id=1, replica_groups=mesh['tensor'=4,'dp'=4,'replica'=2] {'tensor','dp','replica'}, use_global_device_ids=true, to_apply=%region_20.21 | all-reduce | flops 1 | bytes 8 | tf_op jit(solution)/shard_map/psum | solution.py:86
  898.7 9.8 %multiply_convert_fusion = bf16[512,7168]{1,0:T(8,128)(2,1)} fusion(f32[512,7168]{1,0:T(8,128)} %get-tuple-element.26, f32[]{:T(128)S(6)} %rsqrt.75), kind=kLoop, calls=%fused_computation | loop fusion | flops 7340032 | bytes 22020100 | tf_op jit(solution)/shard_map/convert_element_type | solution.py:87
  908.5 16.9 %reshape.113 = bf16[512,2,3584]{2,1,0:T(2,128)(2,1)} reshape(bf16[512,7168]{1,0:T(8,128)(2,1)} %multiply_convert_fusion) | data formatting | bytes 14680064 | tf_op jit(solution)/shard_map/reshape | solution.py:88
  (68 shorter events, 34.0 us)
Async XLA Ops:
  7.2 89.3 %all-gather.3.cloned.1.call-start = ((), (), s32[]{:S(2)}) async-start(), calls=%async_computation.1 | async-start | bytes 88080384 | tf_op jit(solution)/shard_map/all_gather | solution.py:41
  7.9 4.6 copy-start.1
  7.9 4.6 copy-start.2
  7.9 214.9 %all-reduce.10.cloned.1.call-start = ((), (), s32[]{:S(2)}) async-start(), calls=%async_computation.2 | async-start | bytes 1048576 | tf_op jit(solution)/shard_map/psum | solution.py:63
  96.4 39.3 %copy-start.5 = (f32[4096]{0:T(1024)S(1)}, f32[4096]{0:T(1024)}, u32[]{:S(2)}) copy-start(f32[4096]{0:T(1024)} %param.9) | copy-start | bytes 49156
  183.2 61.9 %copy-start.6 = (f32[3]{0:T(128)S(1)}, f32[3]{0:T(128)}, u32[]{:S(2)}) copy-start(f32[3]{0:T(128)} %param.13) | copy-start | bytes 40
  183.3 61.8 %all-reduce.12.cloned.1.call-start = ((), (), s32[]{:S(2)}) async-start(), calls=%async_computation.3 | async-start | bytes 1048576 | tf_op jit(solution)/shard_map/psum | solution.py:65
  226.2 68.6 %all-reduce.14.cloned.1.call-start = ((), (), s32[]{:S(2)}) async-start(), calls=%async_computation.4 | async-start | bytes 1048576 | tf_op jit(solution)/shard_map/psum | solution.py:64
  245.1 138.9 %all-reduce.16.cloned.1.call-start = ((), (), s32[]{:S(2)}) async-start(), calls=%async_computation.5 | async-start | bytes 1048576 | tf_op jit(solution)/shard_map/psum | solution.py:63
  345.5 111.4 %copy-start.4 = (f32[32,4096]{1,0:T(8,128)S(1)}, f32[32,4096]{1,0:T(8,128)}, u32[]{:S(2)}) copy-start(f32[32,4096]{1,0:T(8,128)} %all-reduce.14.cloned.1.call-done) | copy-start | bytes 1572868
  345.5 60.6 %all-reduce.18.cloned.1.call-start = ((), (), s32[]{:S(2)}) async-start(), calls=%async_computation.6 | async-start | bytes 1048576 | tf_op jit(solution)/shard_map/psum | solution.py:65
  387.2 68.4 %all-reduce.20.cloned.1.call-start = ((), (), s32[]{:S(2)}) async-start(), calls=%async_computation.7 | async-start | bytes 1048576 | tf_op jit(solution)/shard_map/psum | solution.py:64
  406.1 139.3 %all-reduce.22.cloned.1.call-start = ((), (), s32[]{:S(2)}) async-start(), calls=%async_computation.8 | async-start | bytes 1048576 | tf_op jit(solution)/shard_map/psum | solution.py:63
  507.0 60.6 %all-reduce.24.cloned.1.call-start = ((), (), s32[]{:S(2)}) async-start(), calls=%async_computation.9 | async-start | bytes 1048576 | tf_op jit(solution)/shard_map/psum | solution.py:65
  548.8 68.5 %all-reduce.26.cloned.1.call-start = ((), (), s32[]{:S(2)}) async-start(), calls=%async_computation.10 | async-start | bytes 1048576 | tf_op jit(solution)/shard_map/psum | solution.py:64
  567.7 264.5 %all-gather.5.cloned.1.call-start = ((), (), s32[]{:S(2)}) async-start(), calls=%async_computation.11 | async-start | bytes 33030144 | tf_op jit(solution)/shard_map/all_gather | solution.py:82
  633.7 3.4 copy-start
  638.9 28.3 %copy-start.3 = (bf16[1,256,3584]{2,1,0:T(8,128)(2,1)S(1)}, bf16[1,256,3584]{2,1,0:T(8,128)(2,1)}, u32[]{:S(2)}) copy-start(bf16[1,256,3584]{2,1,0:T(8,128)(2,1)} %param.11) | copy-start | bytes 5505028
  673.6 46.3 %all-to-all-start = ((bf16[256,8,512]{0,2,1:T(8,128)(2,1)}), bf16[256,8,512]{0,2,1:T(8,128)(2,1)S(1)}, u32[]{:S(2)}, u32[]{:S(2)}) async-start(bf16[256,8,512]{0,2,1:T(8,128)(2,1)} %bitcast.8), calls=%async_computation | async-start | bytes 4194304 | tf_op jit(solution)/shard_map/all_to_all | solution.py:77
Sparse Core Ops, SparseCore 0:
  9.5 86.8 all-gather.2
  183.4 39.4 all-reduce.9
  226.3 18.6 all-reduce.11
  248.2 46.5 all-reduce.13
  345.6 38.2 all-reduce.15
  387.3 18.7 all-reduce.17
  409.1 46.5 all-reduce.19
  507.2 38.2 all-reduce.21
  548.9 18.6 all-reduce.23
  570.8 46.5 all-reduce.25
  673.7 158.3 all-gather.4
